TPU v7x, 32 devices: a whole 2x2x4 slice. The times are simulated.
32 devices in a mesh: line: 1, freq: 4 (over z), section: 2 (over core), rcv: 4 (over y, x).
Axes of the slice: x: 2, y: 2, z: 4, core: 2. Of those that a mesh axis runs over, the one named last changes fastest.
Arguments:
- recorded: bfloat16 [512, 512, 1024], P(('line', 'freq', 'section'), 'rcv'), may hold values from -6 to 6
- signatures: bfloat16 [512, 256], P(('line', 'freq', 'section')), may hold values from -0.375 to 0.375
- ghost_delay: int32 [512, 512], P(('line', 'freq', 'section'), 'rcv'), may hold values from 8 to 47
- dead_trace: int32 [512, 512], P(('line', 'freq', 'section'), 'rcv'), may hold values 0 or 1
Outputs:
- multiples: float32 [2, 32, 512, 512], P(None, ('freq', 'section'), 'line', 'rcv')
All inputs are finite; a program needn't handle non-finite values. No bound on the sum of `dead_trace` on one device may be relied on, other than what follows from the above.
Results may differ from a plain program's by a relative error of at most 0.0041.
Values may be sent and summed in bfloat16 or wider, within the bound.
No kernel may reach another device: no remote copies, remote signals or barrier semaphores. Data moves between devices by JAX's collectives and lax.ppermute only.
A program may use at most 320 MiB of HBM per device.

v0:
```python
import math
import jax
import jax.numpy as jnp
from jax import lax
from jax.sharding import PartitionSpec as P

BIN_DEV = 1
reflectivity = 0.6


def filter_kernel(signatures):
    shot_count, tap_count = signatures.shape
    zero_front = jnp.zeros((shot_count, tap_count), signatures.dtype)
    zero_back = jnp.zeros((shot_count, tap_count + 1), signatures.dtype)
    padded = jnp.concatenate([zero_front, signatures, zero_back], axis=1)
    width = 3 * tap_count
    rows_count = 2 * tap_count
    tiled = jnp.tile(padded, (1, rows_count))[:, : rows_count * width]
    banded = tiled.reshape(shot_count, rows_count, width)
    return banded[:, :, 2 * tap_count :]


def designature(recorded, signatures):
    shot_count, receivers, samples = recorded.shape
    tap_count = signatures.shape[1]
    blocks = samples // tap_count
    kernel = filter_kernel(signatures)
    blocked = recorded.reshape(shot_count, receivers, blocks, tap_count)
    previous_partial = jnp.concatenate(
        [jnp.zeros_like(blocked[:, :, :1]), blocked[:, :, :-1]], axis=2
    )
    window = jnp.concatenate([previous_partial, blocked], axis=3)
    filtered = jnp.einsum("srbj,sji->srbi", window, kernel, preferred_element_type=jnp.float32)
    return filtered.reshape(shot_count, receivers, samples)


def spectrum(filtered, bin_count):
    samples = filtered.shape[2]
    sample_index = jnp.arange(samples, dtype=jnp.int32)
    bin_index = jnp.arange(1, bin_count + 1, dtype=jnp.int32)
    phase_angles = (bin_index[:, None] * sample_index[None, :] % samples).astype(jnp.float32) * (
        2.0 * math.pi / samples
    )
    factor = 1.0 / math.sqrt(samples)
    twiddle = jnp.stack([jnp.cos(phase_angles) * factor, -jnp.sin(phase_angles) * factor])
    return jnp.einsum("srt,pft->pfsr", filtered, twiddle, precision=lax.Precision.HIGHEST)


def deghost(spectra, ghost_delay, dead_trace, samples):
    bin_count = spectra.shape[1]
    bin_index = jnp.arange(1, bin_count + 1, dtype=jnp.int32)
    phase_angles = (bin_index[:, None, None] * ghost_delay[None] % samples).astype(jnp.float32) * (
        2.0 * math.pi / samples
    )
    cosine = jnp.cos(phase_angles)
    sine_value = jnp.sin(phase_angles)
    divisor = 1.0 - 2.0 * reflectivity * cosine + reflectivity * reflectivity
    gain_real = (1.0 - reflectivity * cosine) / divisor
    gain_imag = -reflectivity * sine_value / divisor
    live_mask = (1 - dead_trace).astype(jnp.float32)[None]
    real_part = (spectra[0] * gain_real - spectra[1] * gain_imag) * live_mask
    imag_part = (spectra[0] * gain_imag + spectra[1] * gain_real) * live_mask
    return jnp.stack([real_part, imag_part]).astype(jnp.bfloat16)


def multiply(left_operand, right_operand):
    return jnp.einsum(
        "uxy,uym->uxm", left_operand, right_operand, preferred_element_type=jnp.float32
    )


def complex_product(left_operand, right_operand):
    real_out = multiply(left_operand[0], right_operand[0]) - multiply(
        left_operand[1], right_operand[1]
    )
    imag_out = multiply(left_operand[0], right_operand[1]) + multiply(
        left_operand[1], right_operand[0]
    )
    return jnp.stack([real_out, imag_out])


def per_device(recorded, signatures, ghost_delay, dead_trace):
    samples = recorded.shape[2]
    bin_count = BIN_DEV * lax.axis_size("freq") * lax.axis_size("section") * lax.axis_size("rcv")
    filtered = designature(recorded, signatures)
    spectra = spectrum(filtered, bin_count)
    deghosted = deghost(spectra, ghost_delay, dead_trace, samples)
    relayed = lax.all_to_all(
        deghosted, ("freq", "section"), split_axis=1, concat_axis=2, tiled=True
    )
    summed = complex_product(lax.all_gather(relayed, "rcv", axis=3, tiled=True), relayed)
    station_count = relayed.shape[2]
    return summed * (1.0 / math.sqrt(station_count))


def solution(mesh):
    return jax.shard_map(
        per_device,
        mesh=mesh,
        in_specs=(
            P(("line", "freq", "section"), "rcv", None),
            P(("line", "freq", "section"), None),
            P(("line", "freq", "section"), "rcv"),
            P(("line", "freq", "section"), "rcv"),
        ),
        out_specs=P(None, ("freq", "section"), "line", "rcv"),
        check_vma=False,
    )
```

profile of v0, /device:TPU:0, one launch (start us, length us, event | category | flops | bytes accessed | tf_op | source)
XLA Modules:
  0.0 433.4 jit_solution(421783146112873044)
XLA Ops:
  6.5 0.0 all-gather.2.cloned.1.call-start
  6.5 22.3 %copy.16 = bf16[64,128,1024]{1,2,0:T(8,128)(2,1)} copy(bf16[64,128,1024]{2,1,0:T(8,128)(2,1)} %param.4) | data formatting | bytes 33554432 | tf_op args[0]
  28.8 22.4 %copy.17 = bf16[64,128,4,256]{3,1,2,0:T(8,128)(2,1)} copy(bf16[64,128,4,256]{1,3,2,0:T(8,128)(2,1)} %bitcast.49) | data formatting | bytes 33554432 | tf_op jit(solution)/shard_map/reshape | solution.py:28
  51.2 0.0 copy-start.1
  51.2 10.7 %slice.44 = bf16[64,128,3,256]{3,1,2,0:T(8,128)(2,1)} slice(bf16[64,128,4,256]{3,1,2,0:T(8,128)(2,1)} %copy.17), slice={[0:64], [0:128], [0:3], [0:256]} | slice | bytes 25165824 | tf_op jit(solution)/shard_map/slice | solution.py:30
  62.0 0.0 copy-done.1
  62.0 18.8 %tile.4 = bf16[64,512,769]{2,1,0:T(8,128)(2,1)} broadcast(bf16[64,769]{1,0:T(8,128)(2,1)S(1)} %maximum_maximum_fusion), dimensions={0,2} | broadcast | bytes 50495616 | tf_op jit(solution)/shard_map/tile | solution.py:18
  80.9 122.3 %tile.10 = bf16[64,393728]{1,0:T(8,128)(2,1)} reshape(bf16[64,512,769]{2,1,0:T(8,128)(2,1)} %tile.4) | data formatting | bytes 100794368 | tf_op jit(solution)/shard_map/tile | solution.py:18
  203.2 33.3 %slice.45 = bf16[64,393216]{1,0:T(8,128)(2,1)} slice(bf16[64,393728]{1,0:T(8,128)(2,1)} %tile.10), slice={[0:64], [0:393216]} | slice | bytes 100663296 | tf_op jit(solution)/shard_map/slice | solution.py:18
  236.5 0.0 copy-start.2
  236.5 34.2 %copy.28 = bf16[8,8,512,768]{3,2,1,0:T(8,128)(2,1)} copy(bf16[8,8,512,768]{3,1,2,0:T(8,128)(2,1)} %bitcast.48) | data formatting | bytes 100663296
  270.7 0.6 cosine_multiply_fusion
  271.3 0.0 copy-done.2
  271.3 29.4 %fusion.2 = f32[64,128,4,256]{1,3,2,0:T(8,128)} fusion(bf16[64,128,3,256]{3,1,2,0:T(8,128)(2,1)} %slice.44, bf16[64,128,4,256]{3,1,2,0:T(8,128)(2,1)} %copy.17, bf16[64,512,768]{2,1,0:T(8,128)(2,1)} %bitcast.50), kind=kOutput, calls=%fused_computation.3 | convolution fusion | flops 8690597888 | bytes 79691776 | tf_op jit(solution)/shard_map/srbj,sji->srbi/dot_general | solution.py:33
  300.7 0.0 copy-start
  300.7 24.1 %fusion.20 = f32[2,32,64,128]{3,1,2,0:T(8,128)S(1)} fusion(f32[64,128,1024,1]{1,2,0,3:T(8,128)} %bitcast.51, f32[1,32,1024]{2,1,0:T(8,128)S(1)} %get-tuple-element.12, f32[1,32,1024]{2,1,0:T(8,128)S(1)} %get-tuple-element.11), kind=kOutput, calls=%fused_computation.36 | convolution fusion | flops 6442516480 | bytes 35913728 | tf_op jit(solution)/shard_map/srt,pft->pfsr/dot_general | solution.py:46
  324.8 0.0 copy-done
  324.8 5.1 %multiply_convert_fusion.1 = (bf16[1,32,64,128]{3,1,2,0:T(8,128)(2,1)S(1)}, bf16[1,32,64,128]{3,1,2,0:T(8,128)(2,1)S(1)}) fusion(f32[2,32,64,128]{3,1,2,0:T(8,128)S(1)} %fusion.20, f32[64,128]{1,0:T(8,128)S(1)} %subtract_convert_fusion, s32[64,128]{1,0:T(8,128)S(1)} %copy-done, s32[32]{0:T(128)S(1)} %iota_add_fusion), kind=kLoop, calls=%fused_computation.30 | loop fusion | flops 8126464 | bytes 3211392 | tf_op jit(solution)/shard_map/convert
  329.9 0.1 pad_maximum_fusion
  330.0 0.4 copy.21
  330.4 32.7 %all_to_all.18 = bf16[2,32,64,128]{3,2,0,1:T(8,128)(2,1)S(1)} all-to-all(bf16[2,32,64,128]{3,2,0,1:T(8,128)(2,1)S(1)} %copy.21), channel_id=1, replica_groups=mesh['line'=1,'freq'=4,'section'=2,'rcv'=4] {'freq','section'}, dimensions={1} | all-to-all | bytes 2097152 | tf_op jit(solution)/shard_map/all_to_all | solution.py:88
  363.1 1.1 copy.31
  364.2 0.0 all-gather.2.cloned.1.call-update
  364.2 1.3 fusion.33
  365.5 50.3 %all-gather.2.cloned.1.call-done = bf16[2,4,512,512]{3,2,1,0:T(8,128)(2,1)} async-done(((bf16[2,4,512,128]{3,2,1,0:T(8,128)(2,1)}), bf16[2,4,512,512]{3,2,1,0:T(8,128)(2,1)}) %all-gather.2.cloned.1.call-update) | async-done | bytes 4194320 | tf_op jit(solution)/shard_map/all_gather | solution.py:91
  415.8 2.3 fusion.9
  418.1 2.3 fusion.8
  420.4 2.3 fusion.13
  422.8 2.3 fusion.15
  425.1 1.5 maximum_multiply_fusion
  (7 shorter events, 0.1 us)
Async XLA Ops:
  6.5 409.3 %all-gather.2.cloned.1.call-start = ((), (), s32[]{:S(2)}) async-start(), calls=%async_computation.1 | async-start | bytes 5242880 | tf_op jit(solution)/shard_map/all_gather | solution.py:91
  51.2 10.8 %copy-start.1 = (bf16[64,256]{1,0:T(8,128)(2,1)S(1)}, bf16[64,256]{1,0:T(8,128)(2,1)}, u32[]{:S(2)}) copy-start(bf16[64,256]{1,0:T(8,128)(2,1)} %param.5) | copy-start | bytes 98308
  236.5 34.8 %copy-start.2 = (s32[64,128]{1,0:T(8,128)S(1)}, s32[64,128]{1,0:T(8,128)}, u32[]{:S(2)}) copy-start(s32[64,128]{1,0:T(8,128)} %param.7) | copy-start | bytes 98308
  300.7 24.1 %copy-start = (s32[64,128]{1,0:T(8,128)S(1)}, s32[64,128]{1,0:T(8,128)}, u32[]{:S(2)}) copy-start(s32[64,128]{1,0:T(8,128)} %param.6) | copy-start | bytes 98308
Sparse Core Ops, SparseCore 0:
  364.3 51.4 all-gather.1
where the time goes:
time: 435 us; the launch traced here: 433 us
  local copies, waits for them, and re-layouts  267 us (61%)
  matrix products  62.7 us (14%)
  waiting for transfers between devices  50.3 us (12%)
  blocking collectives  32.7 us (8%)
  between operations  13.5 us (3%)
  other arithmetic  7.29 us (2%)
    another operation x2, local copies, waits for them, and re-layouts, filter_kernel(): tiled = jnp.tile(padded, (1, rows_count))[:, :rows_count * width]  141 us
    unnamed x8, local copies, waits for them, and re-layouts  56.5 us
    all_gather x1, waiting for transfers between devices, per_device(): lax.all_gather(relayed, 'rcv', axis=3, tiled=True)  50.3 us
    slice x1, local copies, waits for them, and re-layouts, filter_kernel(): tiled = jnp.tile(padded, (1, rows_count))[:, :rows_count * width]  33.3 us
    all_to_all x1, blocking collectives, per_device(): lax.all_to_all(deghosted, ('freq', 'section'), split_axis=1, concat_axis=...  32.7 us
    dot_general x1, matrix products, designature(): jnp.einsum('srbj,sji->srbi', window, kernel, preferred_element_type=jnp.f...  29.4 us
    dot_general x1, matrix products, spectrum(): jnp.einsum('srt,pft->pfsr', filtered, twiddle, precision=lax.Precision.HI...  24.1 us
    reshape x1, local copies, waits for them, and re-layouts, designature(): blocked = recorded.reshape(shot_count, receivers, blocks, tap_count)  22.4 us
  transfers between devices with their start and end apart: 1, of which 1 were waited for; matrix products, arithmetic and copies ran while one was open for 0% of the time, Pallas kernels for 0%

commit v1 on v0

--- a/solution.py
+++ b/solution.py
@@ -85,9 +85,18 @@
     filtered = designature(recorded, signatures)
     spectra = spectrum(filtered, bin_count)
     deghosted = deghost(spectra, ghost_delay, dead_trace, samples)
-    relayed = lax.all_to_all(
-        deghosted, ("freq", "section"), split_axis=1, concat_axis=2, tiled=True
-    )
+    a_next, then = (lax.axis_size(("freq", "section")), lax.axis_index(("freq", "section")))
+    new = list(deghosted.shape)
+    piece_out = deghosted.shape[1] // a_next
+    new[1] = piece_out
+    b_next = new[2]
+    new[2] = b_next * a_next
+    relayed = jnp.zeros(new, deghosted.dtype)
+    for j in range(a_next):
+        big = lax.dynamic_slice_in_dim(deghosted, (then ^ j) * piece_out, piece_out, axis=1)
+        if j:
+            big = lax.ppermute(big, ("freq", "section"), [(u, u ^ j) for u in range(a_next)])
+        relayed = lax.dynamic_update_slice_in_dim(relayed, big, (then ^ j) * b_next, axis=2)
     summed = complex_product(lax.all_gather(relayed, "rcv", axis=3, tiled=True), relayed)
     station_count = relayed.shape[2]
     return summed * (1.0 / math.sqrt(station_count))

time: 435 us -> 434 us (level)
  blocking collectives: 32.7 us -> 0 us
  waiting for transfers between devices: 50.3 us -> 72 us
  starting transfers between devices: 0.01 us -> 9.52 us
    all_to_all x1 -> x0, blocking collectives: 32.7 us -> none  [per_device(): lax.all_to_all(deghosted, ('freq', 'section'), split_axis=1, concat_axis=...]
    ppermute x0 -> x7, waiting for transfers between devices: none -> 13.8 us  [per_device(): lax.ppermute(big, ('freq', 'section'), [(u, u ^ j) for u in range(a_next)])]
    ppermute x0 -> x7, starting transfers between devices: none -> 9.52 us  [per_device(): lax.ppermute(big, ('freq', 'section'), [(u, u ^ j) for u in range(a_next)])]
    all_gather x1, waiting for transfers between devices: 50.3 us -> 58.2 us  [per_device(): lax.all_gather(relayed, 'rcv', axis=3, tiled=True)]
    unnamed x8 -> x10, local copies, waits for them, and re-layouts: 56.5 us -> 57.4 us
  transfers between devices with their start and end apart: 1 -> 8, of which waited for: 1 -> 4; matrix products, arithmetic and copies ran while one was open for 0% -> 0% of each run, Pallas kernels for 0% -> 0%
where the time goes in v1:
time: 434 us; the launch traced here: 432 us
  local copies, waits for them, and re-layouts  265 us (61%)
  waiting for transfers between devices  72 us (17%)
  matrix products  63 us (15%)
  between operations  13.6 us (3%)
  starting transfers between devices  9.52 us (2%)
  other arithmetic  8.52 us (2%)
    another operation x2, local copies, waits for them, and re-layouts, filter_kernel(): tiled = jnp.tile(padded, (1, rows_count))[:, :rows_count * width]  141 us
    all_gather x1, waiting for transfers between devices, per_device(): lax.all_gather(relayed, 'rcv', axis=3, tiled=True)  58.2 us
    unnamed x10, local copies, waits for them, and re-layouts  57.4 us
    slice x1, local copies, waits for them, and re-layouts, filter_kernel(): tiled = jnp.tile(padded, (1, rows_count))[:, :rows_count * width]  33.3 us
    dot_general x1, matrix products, designature(): jnp.einsum('srbj,sji->srbi', window, kernel, preferred_element_type=jnp.f...  29.4 us
    dot_general x1, matrix products, spectrum(): jnp.einsum('srt,pft->pfsr', filtered, twiddle, precision=lax.Precision.HI...  24.1 us
    reshape x1, local copies, waits for them, and re-layouts, designature(): blocked = recorded.reshape(shot_count, receivers, blocks, tap_count)  22.4 us
    ppermute x7, waiting for transfers between devices, per_device(): lax.ppermute(big, ('freq', 'section'), [(u, u ^ j) for u in range(a_next)])  13.8 us
  transfers between devices with their start and end apart: 8, of which 4 were waited for; matrix products, arithmetic and copies ran while one was open for 0% of the time, Pallas kernels for 0%

profile of v1, /device:TPU:0, one launch (start us, length us, event | category | flops | bytes accessed | tf_op | source)
XLA Modules:
  0.0 432.1 jit_solution(8157966442795181447)
XLA Ops:
  6.5 0.0 all-gather.2.cloned.1.call-start
  6.5 22.3 %copy.13 = bf16[64,128,1024]{1,2,0:T(8,128)(2,1)} copy(bf16[64,128,1024]{2,1,0:T(8,128)(2,1)} %param.4) | data formatting | bytes 33554432 | tf_op args[0]
  28.8 22.4 %copy.14 = bf16[64,128,4,256]{3,1,2,0:T(8,128)(2,1)} copy(bf16[64,128,4,256]{1,3,2,0:T(8,128)(2,1)} %bitcast.46) | data formatting | bytes 33554432 | tf_op jit(solution)/shard_map/reshape | solution.py:28
  51.2 0.0 copy-start.2
  51.2 10.6 %slice.42 = bf16[64,128,3,256]{3,1,2,0:T(8,128)(2,1)} slice(bf16[64,128,4,256]{3,1,2,0:T(8,128)(2,1)} %copy.14), slice={[0:64], [0:128], [0:3], [0:256]} | slice | bytes 25165824 | tf_op jit(solution)/shard_map/slice | solution.py:30
  61.9 0.0 copy-done.2
  61.9 18.8 %tile.4 = bf16[64,512,769]{2,1,0:T(8,128)(2,1)} broadcast(bf16[64,769]{1,0:T(8,128)(2,1)S(1)} %maximum_maximum_fusion), dimensions={0,2} | broadcast | bytes 50495616 | tf_op jit(solution)/shard_map/tile | solution.py:18
  80.7 122.4 %tile.10 = bf16[64,393728]{1,0:T(8,128)(2,1)} reshape(bf16[64,512,769]{2,1,0:T(8,128)(2,1)} %tile.4) | data formatting | bytes 100794368 | tf_op jit(solution)/shard_map/tile | solution.py:18
  203.0 33.3 %slice.43 = bf16[64,393216]{1,0:T(8,128)(2,1)} slice(bf16[64,393728]{1,0:T(8,128)(2,1)} %tile.10), slice={[0:64], [0:393216]} | slice | bytes 100663296 | tf_op jit(solution)/shard_map/slice | solution.py:18
  236.4 0.0 copy-start.3
  236.4 34.2 %copy.31 = bf16[8,8,512,768]{3,2,1,0:T(8,128)(2,1)} copy(bf16[8,8,512,768]{3,1,2,0:T(8,128)(2,1)} %bitcast.45) | data formatting | bytes 100663296
  270.5 0.6 cosine_multiply_fusion
  271.1 0.0 copy-done.3
  271.2 29.4 %fusion.2 = f32[64,128,4,256]{1,3,2,0:T(8,128)} fusion(bf16[64,128,3,256]{3,1,2,0:T(8,128)(2,1)} %slice.42, bf16[64,128,4,256]{3,1,2,0:T(8,128)(2,1)} %copy.14, bf16[64,512,768]{2,1,0:T(8,128)(2,1)} %bitcast.47), kind=kOutput, calls=%fused_computation.3 | convolution fusion | flops 8690597888 | bytes 79691776 | tf_op jit(solution)/shard_map/srbj,sji->srbi/dot_general | solution.py:33
  300.6 0.0 copy-start.1
  300.6 24.1 %fusion.20 = f32[2,32,64,128]{3,1,2,0:T(8,128)S(1)} fusion(f32[64,128,1024,1]{1,2,0,3:T(8,128)} %bitcast.48, f32[1,32,1024]{2,1,0:T(8,128)S(1)} %get-tuple-element.16, f32[1,32,1024]{2,1,0:T(8,128)S(1)} %get-tuple-element.15), kind=kOutput, calls=%fused_computation.53 | convolution fusion | flops 6442516480 | bytes 35913728 | tf_op jit(solution)/shard_map/srt,pft->pfsr/dot_general | solution.py:46
  324.7 0.0 copy-done.1
  324.7 5.1 %multiply_convert_fusion = (bf16[1,32,64,128]{3,1,2,0:T(8,128)(2,1)S(1)}, bf16[1,32,64,128]{3,1,2,0:T(8,128)(2,1)S(1)}) fusion(f32[2,32,64,128]{3,1,2,0:T(8,128)S(1)} %fusion.20, f32[64,128]{1,0:T(8,128)S(1)} %subtract_convert_fusion, s32[64,128]{1,0:T(8,128)S(1)} %copy-done.1, s32[32]{0:T(128)S(1)} %iota_add_fusion), kind=kLoop, calls=%fused_computation.44 | loop fusion | flops 8126464 | bytes 3211392 | tf_op jit(solution)/shard_map/convert.1
  329.8 1.2 fusion.23
  331.0 0.5 collective-permute-start
  331.4 2.6 collective-permute-start.1
  334.0 0.1 collective-permute-start.2
  334.1 2.7 collective-permute-start.3
  336.9 0.1 fusion.30
  337.0 0.1 collective-permute-start.4
  337.1 0.1 broadcast_in_dim.6
  337.3 0.0 collective-permute-done
  337.3 3.5 collective-permute-start.5
  340.9 2.8 collective-permute-done.1
  343.8 0.0 collective-permute-start.6
  343.8 2.5 collective-permute-done.2
  346.3 0.0 collective-permute-done.3
  346.4 8.4 %collective-permute-done.4 = bf16[2,4,64,128]{3,1,2,0:T(4,128)(2,1)S(1)} collective-permute-done((bf16[2,4,64,128]{3,1,2,0:T(4,128)(2,1)S(1)}, bf16[2,4,64,128]{3,1,2,0:T(4,128)(2,1)S(1)}, u32[]{:S(2)}, u32[]{:S(2)}) %collective-permute-start.4) | collective-permute-done | bytes 131104 | tf_op jit(solution)/shard_map/ppermute | solution.py:98
  354.8 0.0 collective-permute-done.5
  354.9 0.0 collective-permute-done.6
  355.0 0.0 copy-start
  355.0 1.0 copy-done
  355.9 0.0 all-gather.2.cloned.1.call-update
  356.0 58.2 %all-gather.2.cloned.1.call-done = bf16[2,4,512,512]{3,2,1,0:T(8,128)(2,1)} async-done(((bf16[2,4,512,128]{3,2,1,0:T(8,128)(2,1)}), bf16[2,4,512,512]{3,2,1,0:T(8,128)(2,1)}) %all-gather.2.cloned.1.call-update) | async-done | bytes 4194320 | tf_op jit(solution)/shard_map/all_gather | solution.py:100
  414.1 2.4 fusion.11
  416.5 2.4 fusion.10
  418.9 2.4 fusion.13
  421.3 2.4 fusion.15
  423.7 1.5 maximum_multiply_fusion
  (15 shorter events, 0.4 us)
Async XLA Ops:
  6.5 407.6 %all-gather.2.cloned.1.call-start = ((), (), s32[]{:S(2)}) async-start(), calls=%async_computation | async-start | bytes 5242880 | tf_op jit(solution)/shard_map/all_gather | solution.py:100
  51.2 10.7 %copy-start.2 = (bf16[64,256]{1,0:T(8,128)(2,1)S(1)}, bf16[64,256]{1,0:T(8,128)(2,1)}, u32[]{:S(2)}) copy-start(bf16[64,256]{1,0:T(8,128)(2,1)} %param.5) | copy-start | bytes 98308
  236.4 34.8 %copy-start.3 = (s32[64,128]{1,0:T(8,128)S(1)}, s32[64,128]{1,0:T(8,128)}, u32[]{:S(2)}) copy-start(s32[64,128]{1,0:T(8,128)} %param.7) | copy-start | bytes 98308
  300.6 24.1 %copy-start.1 = (s32[64,128]{1,0:T(8,128)S(1)}, s32[64,128]{1,0:T(8,128)}, u32[]{:S(2)}) copy-start(s32[64,128]{1,0:T(8,128)} %param.6) | copy-start | bytes 98308
  331.0 6.4 %collective-permute-start = (bf16[2,4,64,128]{3,1,2,0:T(4,128)(2,1)}, bf16[2,4,64,128]{3,1,2,0:T(4,128)(2,1)S(1)}, u32[]{:S(2)}, u32[]{:S(2)}) collective-permute-start(bf16[2,4,64,128]{3,1,2,0:T(4,128)(2,1)} %get-tuple-element.9), channel_id=1, source_target_pairs={{0,4},{4,0},{8,12},{12,8},{16,20},{20,16},{24,28},{28,24},{1,5},{5... | collective-permute-start | bytes 393224 | tf_op jit(solution)/shard_map/ppermute | solution.py:98
  331.4 12.3 %collective-permute-start.1 = (bf16[2,4,64,128]{3,1,2,0:T(4,128)(2,1)}, bf16[2,4,64,128]{3,1,2,0:T(4,128)(2,1)S(1)}, u32[]{:S(2)}, u32[]{:S(2)}) collective-permute-start(bf16[2,4,64,128]{3,1,2,0:T(4,128)(2,1)} %get-tuple-element.10), channel_id=1, source_target_pairs={{0,8},{4,12},{8,0},{12,4},{16,24},{20,28},{24,16},{28,20},{1,9},{5... | collective-permute-start | bytes 393224 | tf_op jit(solution)/shard_map/ppermute | solution.py:98
  334.0 12.3 %collective-permute-start.2 = (bf16[2,4,64,128]{3,1,2,0:T(4,128)(2,1)S(1)}, bf16[2,4,64,128]{3,1,2,0:T(4,128)(2,1)S(1)}, u32[]{:S(2)}, u32[]{:S(2)}) collective-permute-start(bf16[2,4,64,128]{3,1,2,0:T(4,128)(2,1)S(1)} %get-tuple-element.11), channel_id=1, source_target_pairs={{0,12},{4,8},{8,4},{12,0},{16,28},{20,24},{24,20},{28,16},{1,13},{... | collective-permute-start | bytes 393224 | tf_op jit(solution)/shard_map/ppermute | solution.py:98
  334.1 12.2 %collective-permute-start.3 = (bf16[2,4,64,128]{3,1,2,0:T(4,128)(2,1)S(1)}, bf16[2,4,64,128]{3,1,2,0:T(4,128)(2,1)S(1)}, u32[]{:S(2)}, u32[]{:S(2)}) collective-permute-start(bf16[2,4,64,128]{3,1,2,0:T(4,128)(2,1)S(1)} %get-tuple-element.12), channel_id=1, source_target_pairs={{0,16},{4,20},{8,24},{12,28},{16,0},{20,4},{24,8},{28,12},{1,17},{... | collective-permute-start | bytes 393224 | tf_op jit(solution)/shard_map/ppermute | solution.py:98
  337.0 17.8 %collective-permute-start.4 = (bf16[2,4,64,128]{3,1,2,0:T(4,128)(2,1)S(1)}, bf16[2,4,64,128]{3,1,2,0:T(4,128)(2,1)S(1)}, u32[]{:S(2)}, u32[]{:S(2)}) collective-permute-start(bf16[2,4,64,128]{3,1,2,0:T(4,128)(2,1)S(1)} %get-tuple-element.14), channel_id=1, source_target_pairs={{0,20},{4,16},{8,28},{12,24},{16,4},{20,0},{24,12},{28,8},{1,21},{... | collective-permute-start | bytes 393224 | tf_op jit(solution)/shard_map/ppermute | solution.py:98
  337.3 17.5 %collective-permute-start.5 = (bf16[2,4,64,128]{3,1,2,0:T(4,128)(2,1)S(1)}, bf16[2,4,64,128]{3,1,2,0:T(4,128)(2,1)S(1)}, u32[]{:S(2)}, u32[]{:S(2)}) collective-permute-start(bf16[2,4,64,128]{3,1,2,0:T(4,128)(2,1)S(1)} %get-tuple-element.13), channel_id=1, source_target_pairs={{0,24},{4,28},{8,16},{12,20},{16,8},{20,12},{24,0},{28,4},{1,25},{... | collective-permute-start | bytes 393224 | tf_op jit(solution)/shard_map/ppermute | solution.py:98
  343.8 11.1 %collective-permute-start.6 = (bf16[2,4,64,128]{3,1,2,0:T(4,128)(2,1)S(1)}, bf16[2,4,64,128]{3,1,2,0:T(4,128)(2,1)S(1)}, u32[]{:S(2)}, u32[]{:S(2)}) collective-permute-start(bf16[2,4,64,128]{3,1,2,0:T(4,128)(2,1)S(1)} %get-tuple-element.7), channel_id=1, source_target_pairs={{0,28},{4,24},{8,20},{12,16},{16,12},{20,8},{24,4},{28,0},{1,29},{... | collective-permute-start | bytes 393224 | tf_op jit(solution)/shard_map/ppermute | solution.py:98
  355.0 1.0 copy-start
Sparse Core Ops, SparseCore 0:
  356.1 58.0 all-gather.1
